TPU v7x, 256 devices: a whole 4x4x8 slice. The times are simulated.
256 devices in a mesh: layer: 8 (over y_lo, x), prow: 4 (over y_hi, core), pcol: 8 (over z).
Axes of the slice: x: 4, y: 4 (y_hi: 2, y_lo: 2; y = y_hi * 2 + y_lo), z: 8, core: 2. Of those that a mesh axis runs over, the one named last changes fastest.
Arguments:
- front_blocks: float32 [8, 4, 1024, 4, 1024], P('layer', None, 'prow', None, 'pcol'), may hold values from -6 to 6, as said below
- fill_mask: int32 [32, 32], replicated, may hold values from 0 to 1, as said below
Outputs:
- factored: float32 [8, 4, 1024, 4, 1024], P('layer', None, 'prow', None, 'pcol')
- ancestor: float32 [3, 4, 8, 32, 3, 1024], P(None, 'prow', 'layer', None, None, 'pcol')
Inputs may be any that keep to these rules, and one draw needn't show every extreme that they name: `front_blocks`: with the fill pattern applied, every pivot block that the elimination meets is invertible and well conditioned. `fill_mask`: block row i is filled exactly from some block column at most i // 2 through the diagonal block, and block column j exactly from some block row at most j // 2 through the diagonal block; all other block pairs are empty.
All inputs are finite; a program needn't handle non-finite values.
Results may differ from a plain program's by a relative error of at most 0.0001.
Values sent between devices are 32-bit elements; how exact they have to be, the bound alone decides.
A program may use at most 128 MiB of HBM per device.

v0:
```python
import jax
import jax.numpy as jnp
from jax import lax
from jax.sharding import Mesh
from jax.sharding import PartitionSpec as P

P_SIZE = 1024
BS = 128
PANELS = 1
PROW = ("prow_0", "prow_1")
PROW_PCOL = ("prow_0", "prow_1", "pcol")


def edges_of(length, count):
    lap = length // count
    if lap >= 8:
        lap -= lap % 8
    return [lap * k for k in range(1, count)]


def all_blocks(shard, axes, order):
    tiles = shard[None]
    for k in order:
        tiles = lax.all_gather(tiles, axes[k], axis=0, tiled=True)
    block = [lax.axis_size(axes[k]) for k in reversed(order)]
    tiles = tiles.reshape(*block, *shard.shape)
    turned = sorted(range(len(order)), key=lambda place: order[len(order) - 1 - place])
    return tiles.transpose(*turned, *range(len(order), tiles.ndim)).reshape(-1, *shard.shape)


def joined_along(tiles, dim):
    tiles = jnp.moveaxis(tiles, 0, dim)
    shape = tiles.shape
    return tiles.reshape(*shape[:dim], shape[dim] * shape[dim + 1], *shape[dim + 2 :])


def gather_all_axes(shard, axes, dim):
    numbers = list(range(len(axes)))[::-1]
    widest = shard.shape.index(max(shard.shape[:-1] or shard.shape))
    edges = [0, *edges_of(shard.shape[widest], len(axes)), shard.shape[widest]]
    finished = []
    for k, (start, end) in enumerate(zip(edges, edges[1:])):
        if end > start:
            share = lax.slice_in_dim(shard, start, end, axis=widest)
            finished.append(all_blocks(share, axes, numbers[k:] + numbers[:k]))
    return joined_along(jnp.concatenate(finished, axis=widest + 1), dim)


def sent_to_all(shard, axis):
    copies = jnp.broadcast_to(shard, (lax.axis_size(axis), *shard.shape))
    return lax.all_to_all(copies, axis, split_axis=0, concat_axis=0, tiled=True)


def gathered_copies(shard, axis, dim):
    tiles = sent_to_all(shard, axis)
    return joined_along(tiles, dim)


def cut_along(shard, dim, length):
    shape = shard.shape
    tiles = shard.reshape(*shape[:dim], length, shape[dim] // length, *shape[dim + 1 :])
    return jnp.moveaxis(tiles, dim, 0)


def summed_on_arrival(shard, axis, dim):
    length = lax.axis_size(axis)
    tiles = lax.all_to_all(cut_along(shard, dim, length), axis, 0, 0, tiled=True)
    return jnp.sum(tiles, axis=0)


def full_dot(left, right):
    return jnp.dot(left, right, precision=lax.Precision.HIGHEST, preferred_element_type=jnp.float32)


def invert(pivot_tile):
    gram_matrix = full_dot(pivot_tile.T, pivot_tile)
    cholesky_factor = jnp.linalg.cholesky(gram_matrix)
    return jax.scipy.linalg.cho_solve((cholesky_factor, True), pivot_tile.T)


def factor_pivot(matrix):
    pieces = []
    remainder = matrix
    for position in range(matrix.shape[0] // BS):
        pivot_tile = remainder[:BS, :BS]
        inverse = invert(pivot_tile)
        lower_part = full_dot(remainder[BS:, :BS], inverse)
        upper_part = remainder[:BS, BS:]
        pieces.append((pivot_tile, inverse, lower_part, upper_part))
        remainder = remainder[BS:, BS:] - full_dot(lower_part, upper_part)
    return pieces


def assemble(pieces):
    columns_list = []
    for column, piece in enumerate(pieces):
        above_part = [
            pieces[earlier][3][:, (column - earlier - 1) * BS : (column - earlier) * BS]
            for earlier in range(column)
        ]
        columns_list.append(jnp.concatenate(above_part + [piece[0], piece[2]], axis=0))
    return jnp.concatenate(columns_list, axis=1)


def solve_lower(row_data, pieces):
    results = []
    remaining_cols = row_data
    for pivot_tile, inverse, lower_part, upper_part in pieces:
        solved = full_dot(remaining_cols[:, :BS], inverse)
        results.append(solved)
        remaining_cols = remaining_cols[:, BS:] - full_dot(solved, upper_part)
    return jnp.concatenate(results, axis=1)


def solve_upper(column_data, pieces):
    results = []
    remaining_rows = column_data
    for pivot_tile, inverse, lower_part, upper_part in pieces:
        leading = remaining_rows[:BS]
        results.append(leading)
        remaining_rows = remaining_rows[BS:] - full_dot(lower_part, leading)
    return jnp.concatenate(results, axis=0)


def on_device(front_blocks, fill_mask):
    grid_row = lax.axis_index(PROW)
    grid_col = lax.axis_index("pcol")
    row_groups = lax.axis_size(PROW)
    col_groups = lax.axis_size("pcol")
    supers = front_blocks.shape[1]
    rows_dev = front_blocks.shape[2]
    cols_dev = front_blocks.shape[4]
    blocks_row = rows_dev // BS
    blocks_col = cols_dev // BS
    fill_table = fill_mask.reshape(supers, P_SIZE // BS, supers, P_SIZE // BS)
    fill_table = lax.dynamic_slice(
        fill_table,
        (0, grid_row * blocks_row, 0, grid_col * blocks_col),
        (supers, blocks_row, supers, blocks_col),
    )
    fill_table = jnp.broadcast_to(
        fill_table[:, :, None, :, :, None], (supers, blocks_row, BS, supers, blocks_col, BS)
    )
    fill_table = fill_table.reshape(supers, rows_dev, supers, cols_dev).astype(jnp.float32)
    current = front_blocks[0] * fill_table
    remaining = supers - 1
    own_tile = current[0, :, 0, :]
    gathered = gather_all_axes(own_tile[None], PROW_PCOL, 0)
    pivot_full = (
        gathered.reshape(row_groups, col_groups, rows_dev, cols_dev)
        .transpose(0, 2, 1, 3)
        .reshape(P_SIZE, P_SIZE)
    )
    pieces = factor_pivot(pivot_full)
    upper_rows = gathered_copies(current[0, :, 1:, :], PROW, 0)
    solved_upper = solve_upper(upper_rows.reshape(P_SIZE, remaining * cols_dev), pieces)
    below_part = current[1:, :, 0, :]
    widened = lax.all_gather(below_part, "pcol", axis=2, tiled=True)
    lower_rows = solve_lower(widened.reshape(remaining * rows_dev, P_SIZE), pieces).reshape(
        remaining, rows_dev, P_SIZE
    )
    factored_pivot = assemble(pieces)
    own_pivot = lax.dynamic_slice(
        factored_pivot, (grid_row * rows_dev, grid_col * cols_dev), (rows_dev, cols_dev)
    )
    own_upper = lax.dynamic_slice_in_dim(solved_upper, grid_row * rows_dev, rows_dev, 0).reshape(
        rows_dev, remaining, cols_dev
    )
    own_lower = lax.dynamic_slice_in_dim(lower_rows, grid_col * cols_dev, cols_dev, 2)
    update_term = full_dot(lower_rows.reshape(remaining * rows_dev, P_SIZE), solved_upper)
    trailing = current[1:, :, 1:, :] - update_term.reshape(remaining, rows_dev, remaining, cols_dev)
    current = current.at[0, :, 0, :].set(own_pivot)
    current = current.at[0, :, 1:, :].set(own_upper)
    current = current.at[1:, :, 0, :].set(own_lower)
    current = current.at[1:, :, 1:, :].set(trailing)
    trailing_own = current[PANELS:, :, PANELS:, :]
    summed = summed_on_arrival(trailing_own, "layer", 1)
    ancestor_rows = summed.shape[1]
    ancestor_part = summed.reshape(supers - PANELS, 1, 1, ancestor_rows, supers - PANELS, cols_dev)
    return (current[None], ancestor_part)


def solution(mesh):
    torus = Mesh(
        mesh.devices.reshape(mesh.shape["layer"], 2, 2, mesh.shape["pcol"]),
        ("layer", "prow_0", "prow_1", "pcol"),
    )
    placed = (P("layer", None, PROW, None, "pcol"), P())
    return jax.shard_map(
        on_device,
        mesh=torus,
        in_specs=placed,
        out_specs=(
            P("layer", None, PROW, None, "pcol"),
            P(None, PROW, "layer", None, None, "pcol"),
        ),
        check_vma=False,
    )
```

profile of v0, /device:TPU:16, one launch (start us, length us, event | category | flops | bytes accessed | tf_op | source)
XLA Modules:
  0.0 525.2 jit_solution(7103626663641285439)
XLA Ops:
  7.2 2.9 copy.63
  12.7 28.7 %all-gather = f32[8,80,128]{2,1,0:T(8,128)S(1)} all-gather(f32[1,80,128]{2,1,0:T(8,128)S(1)} %copy.66), channel_id=2, replica_groups=mesh['layer'=8,'prow_0'=2,'prow_1'=2,'pcol'=8] {'pcol'}, dimensions={0}, use_global_device_ids=true | all-gather | bytes 368640 | tf_op jit(solution)/shard_map/all_gather | solution.py:24
  41.4 2.4 all-gather.1
  44.1 6.3 %all-gather.6 = f32[2,96,128]{2,1,0:T(8,128)S(1)} all-gather(f32[1,96,128]{2,1,0:T(8,128)S(1)} %copy.69), channel_id=8, replica_groups=mesh['layer'=8,'prow_0'=2,'prow_1'=2,'pcol'=8] {'prow_0'}, dimensions={0}, use_global_device_ids=true | all-gather | bytes 147456 | tf_op jit(solution)/shard_map/all_gather | solution.py:24
  50.3 28.1 %all-gather.7 = f32[16,96,128]{2,1,0:T(8,128)} all-gather(f32[2,96,128]{2,1,0:T(8,128)S(1)} %all-gather.6), channel_id=9, replica_groups=mesh['layer'=8,'prow_0'=2,'prow_1'=2,'pcol'=8] {'pcol'}, dimensions={0}, use_global_device_ids=true | all-gather | bytes 884736 | tf_op jit(solution)/shard_map/all_gather | solution.py:24
  80.4 6.8 %all-gather.4 = f32[4,80,128]{2,1,0:T(8,128)} all-gather(f32[2,80,128]{2,1,0:T(8,128)S(1)} %all-gather.3), channel_id=6, replica_groups=mesh['layer'=8,'prow_0'=2,'prow_1'=2,'pcol'=8] {'prow_0'}, dimensions={0}, use_global_device_ids=true | all-gather | bytes 245760 | tf_op jit(solution)/shard_map/all_gather | solution.py:24
  88.6 4.8 all-to-all-start
  96.2 15.7 %all-to-all-done = f32[4,256,3,128]{1,3,2,0:T(8,128)} async-done(((f32[4,256,3,128]{1,3,2,0:T(8,128)}), f32[4,256,3,128]{1,3,2,0:T(8,128)}, u32[]{:S(2)}, u32[]{:S(2)}) %all-to-all-start) | async-done | bytes 1572896 | tf_op jit(solution)/shard_map/all_to_all | solution.py:51
  111.9 2.1 copy.92
  117.8 2.3 copy.70
  120.1 15.3 %all-gather.17.cloned.1.call-done = f32[32,80,128]{2,1,0:T(8,128)} async-done(((f32[4,80,128]{2,1,0:T(8,128)}), f32[32,80,128]{2,1,0:T(8,128)}) %all-gather.17.cloned.1.call-update) | async-done | bytes 1310736 | tf_op jit(solution)/shard_map/all_gather | solution.py:24
  135.4 2.1 copy.68
  141.1 11.7 %cholesky.134 = f32[128,128]{1,0:T(8,128)S(1)} custom-call(f32[128,128]{1,0:T(8,128)S(1)} %fusion.103), custom_call_target="Cholesky" | custom-call | tf_op jit(solution)/shard_map/jit(cholesky)/cholesky | solution.py:77
  154.2 9.8 %custom-call.14 = f32[1,128,128]{1,2,0:T(8,128)S(1)} custom-call(f32[1,128,128]{2,1,0:T(8,128)S(1)} %fusion.46), custom_call_target="InvertDiagBlocksLowerTriangular" | custom-call | tf_op jit(solution)/shard_map/jit(_cho_solve)/triangular_solve | solution.py:78
  168.3 5.2 slice_subtract_fusion
  175.8 11.7 %cholesky.145 = f32[128,128]{1,0:T(8,128)S(1)} custom-call(f32[128,128]{1,0:T(8,128)S(1)} %fusion.97), custom_call_target="Cholesky" | custom-call | tf_op jit(solution)/shard_map/jit(cholesky)/cholesky | solution.py:77
  188.8 9.8 %custom-call.15 = f32[1,128,128]{1,2,0:T(8,128)S(1)} custom-call(f32[1,128,128]{2,1,0:T(8,128)S(1)} %fusion.47), custom_call_target="InvertDiagBlocksLowerTriangular" | custom-call | tf_op jit(solution)/shard_map/jit(_cho_solve)/triangular_solve | solution.py:78
  200.3 2.0 slice_subtract_fusion.3
  205.4 11.9 %cholesky.156 = f32[128,128]{1,0:T(8,128)S(1)} custom-call(f32[128,128]{1,0:T(8,128)S(1)} %fusion.91), custom_call_target="Cholesky" | custom-call | tf_op jit(solution)/shard_map/jit(cholesky)/cholesky | solution.py:77
  218.7 9.8 %custom-call.16 = f32[1,128,128]{1,2,0:T(8,128)S(1)} custom-call(f32[1,128,128]{2,1,0:T(8,128)S(1)} %fusion.48), custom_call_target="InvertDiagBlocksLowerTriangular" | custom-call | tf_op jit(solution)/shard_map/jit(_cho_solve)/triangular_solve | solution.py:78
  231.9 3.0 slice_subtract_fusion.5
  246.8 13.2 %cholesky.167 = f32[128,128]{1,0:T(8,128)} custom-call(f32[128,128]{1,0:T(8,128)} %fusion.85), custom_call_target="Cholesky" | custom-call | tf_op jit(solution)/shard_map/jit(cholesky)/cholesky | solution.py:77
  261.5 2.2 fusion.49
  263.7 11.4 %custom-call.17 = f32[1,128,128]{1,2,0:T(8,128)} custom-call(f32[1,128,128]{2,1,0:T(8,128)} %fusion.49), custom_call_target="InvertDiagBlocksLowerTriangular" | custom-call | tf_op jit(solution)/shard_map/jit(_cho_solve)/triangular_solve | solution.py:78
  277.4 2.1 constant_dynamic-update-slice_fusion.10
  284.6 2.3 convolution_subtract_fusion.3
  291.6 13.2 %cholesky.178 = f32[128,128]{1,0:T(8,128)} custom-call(f32[128,128]{1,0:T(8,128)} %fusion.79), custom_call_target="Cholesky" | custom-call | tf_op jit(solution)/shard_map/jit(cholesky)/cholesky | solution.py:77
  306.3 2.1 fusion.50
  308.4 11.3 %custom-call.18 = f32[1,128,128]{1,2,0:T(8,128)} custom-call(f32[1,128,128]{2,1,0:T(8,128)} %fusion.50), custom_call_target="InvertDiagBlocksLowerTriangular" | custom-call | tf_op jit(solution)/shard_map/jit(_cho_solve)/triangular_solve | solution.py:78
  333.3 12.1 %cholesky.189 = f32[128,128]{1,0:T(8,128)S(1)} custom-call(f32[128,128]{1,0:T(8,128)S(1)} %fusion.73), custom_call_target="Cholesky" | custom-call | tf_op jit(solution)/shard_map/jit(cholesky)/cholesky | solution.py:77
  346.8 9.8 %custom-call.19 = f32[1,128,128]{1,2,0:T(8,128)S(1)} custom-call(f32[1,128,128]{2,1,0:T(8,128)S(1)} %fusion.51), custom_call_target="InvertDiagBlocksLowerTriangular" | custom-call | tf_op jit(solution)/shard_map/jit(_cho_solve)/triangular_solve | solution.py:78
  369.6 12.5 %cholesky.200 = f32[128,128]{1,0:T(8,128)S(1)} custom-call(f32[128,128]{1,0:T(8,128)} %fusion.67), custom_call_target="Cholesky" | custom-call | tf_op jit(solution)/shard_map/jit(cholesky)/cholesky | solution.py:77
  384.3 10.6 %custom-call.20 = f32[1,128,128]{1,2,0:T(8,128)S(1)} custom-call(f32[1,128,128]{2,1,0:T(8,128)} %fusion.52), custom_call_target="InvertDiagBlocksLowerTriangular" | custom-call | tf_op jit(solution)/shard_map/jit(_cho_solve)/triangular_solve | solution.py:78
  414.8 2.7 convolution_subtract_fusion
  423.7 11.7 %cholesky.211 = f32[128,128]{1,0:T(8,128)S(1)} custom-call(f32[128,128]{1,0:T(8,128)S(1)} %fusion.61), custom_call_target="Cholesky" | custom-call | tf_op jit(solution)/shard_map/jit(cholesky)/cholesky | solution.py:77
  436.7 10.0 %custom-call.21 = f32[1,128,128]{1,2,0:T(8,128)S(1)} custom-call(f32[1,128,128]{2,1,0:T(8,128)S(1)} %fusion.53), custom_call_target="InvertDiagBlocksLowerTriangular" | custom-call | tf_op jit(solution)/shard_map/jit(_cho_solve)/triangular_solve | solution.py:78
  447.2 2.1 bitcast_dynamic-update-slice_fusion.2
  449.3 3.5 copy.84
  454.4 4.5 slice_subtract_fusion.1
  459.4 3.2 slice_subtract_fusion.2
  463.2 2.8 slice_subtract_fusion.4
  466.6 2.4 slice_subtract_fusion.6
  469.5 2.1 convolution_subtract_fusion.1
  476.9 2.4 copy.86
  479.3 7.5 %fusion.131 = f32[768,384]{1,0:T(8,128)} fusion(f32[768,1024]{0,1:T(8,128)S(1)} %convolution_dynamic-update-slice_fusion, f32[1024,384]{1,0:T(8,128)} %copy-done.16), kind=kOutput, calls=%fused_computation.254 | convolution fusion | flops 3623878656 | bytes 5898240 | tf_op jit(solution)/shard_map/dot_general | solution.py:72
  488.7 2.9 reshape.233
  499.6 4.9 all-to-all-start.1
  506.4 11.1 %all-to-all-done.1 = f32[8,3,32,3,128]{4,2,3,1,0:T(8,128)S(1)} async-done(((f32[8,3,32,3,128]{4,2,3,1,0:T(8,128)}), f32[8,3,32,3,128]{4,2,3,1,0:T(8,128)S(1)}, u32[]{:S(2)}, u32[]{:S(2)}) %all-to-all-start.1) | async-done | bytes 1179680 | tf_op jit(solution)/shard_map/all_to_all | solution.py:67
  (271 shorter events, 140.7 us)
Async XLA Ops:
  7.2 3.0 copy-start.44
  7.2 108.8 %all-gather.15.cloned.1.call-start = ((), (), s32[]{:S(2)}) async-start(), calls=%async_computation.2 | async-start | bytes 1966080 | tf_op jit(solution)/shard_map/all_gather | solution.py:24
  12.5 81.7 %copy-start = (f32[4,256,4,128]{1,3,2,0:T(8,128)}, f32[4,256,4,128]{1,3,2,0:T(8,128)S(1)}, u32[]{:S(2)}) copy-start(f32[4,256,4,128]{1,3,2,0:T(8,128)S(1)} %bitcast_multiply_fusion) | copy-start | bytes 6291460
  43.8 73.9 %all-gather.19.cloned.1.call-start = ((), (), s32[]{:S(2)}) async-start(), calls=%async_computation.4 | async-start | bytes 2359296 | tf_op jit(solution)/shard_map/all_gather | solution.py:24
  78.4 57.0 %all-gather.17.cloned.1.call-start = ((), (), s32[]{:S(2)}) async-start(), calls=%async_computation.3 | async-start | bytes 1474560 | tf_op jit(solution)/shard_map/all_gather | solution.py:24
  88.6 23.3 %all-to-all-start = ((f32[4,256,3,128]{1,3,2,0:T(8,128)}), f32[4,256,3,128]{1,3,2,0:T(8,128)}, u32[]{:S(2)}, u32[]{:S(2)}) async-start(f32[4,256,3,128]{1,3,2,0:T(8,128)} %broadcast_in_dim.36), calls=%async_computation | async-start | bytes 3145728 | tf_op jit(solution)/shard_map/all_to_all | solution.py:51
  93.4 1.4 copy-start.45
  93.4 356.0 %all-gather.21.cloned.1.call-start = ((), (), s32[]{:S(2)}) async-start(), calls=%async_computation.5 | async-start | bytes 3538944 | tf_op jit(solution)/shard_map/all_gather | solution.py:158
  114.2 1.1 copy-start.18
  138.8 1.9 copy-start.3
  167.5 0.8 copy-start.6
  173.5 151.9 %copy-start.5 = (f32[896,896]{1,0:T(8,128)}, f32[896,896]{1,0:T(8,128)S(1)}, u32[]{:S(2)}) copy-start(f32[896,896]{1,0:T(8,128)S(1)} %slice_subtract_fusion) | copy-start | bytes 9633796
  198.7 5.8 %copy-start.7 = (f32[896,128]{1,0:T(8,128)S(1)}, f32[896,128]{1,0:T(8,128)}, u32[]{:S(2)}) copy-start(f32[896,128]{1,0:T(8,128)} %copy-done.6) | copy-start | bytes 1376260
  200.3 4.2 copy-start.10
  202.3 1.5 copy-start.9
  228.5 6.4 %copy-start.11 = (f32[768,128]{1,0:T(8,128)S(1)}, f32[768,128]{1,0:T(8,128)}, u32[]{:S(2)}) copy-start(f32[768,128]{1,0:T(8,128)} %copy-done.10) | copy-start | bytes 1179652
  228.5 8.3 %copy-start.43 = (f32[128,128]{1,0:T(8,128)S(1)}, f32[128,128]{1,0:T(8,128)}, u32[]{:S(2)}) copy-start(f32[128,128]{1,0:T(8,128)} %slice.541) | copy-start | bytes 196612
  234.9 8.2 %copy-start.13 = (f32[640,640]{1,0:T(8,128)}, f32[640,640]{1,0:T(8,128)S(1)}, u32[]{:S(2)}) copy-start(f32[640,640]{1,0:T(8,128)S(1)} %slice_subtract_fusion.5) | copy-start | bytes 4915204
  277.4 7.2 %copy-start.36 = (f32[128,128]{1,0:T(8,128)}, f32[128,128]{1,0:T(8,128)S(1)}, u32[]{:S(2)}) copy-start(f32[128,128]{1,0:T(8,128)S(1)} %fusion.82) | copy-start | bytes 196612
  279.4 5.1 copy-start.19
  286.9 1.0 copy-start.14
  321.9 8.6 %copy-start.26 = (f32[128,128]{1,0:T(8,128)}, f32[128,128]{1,0:T(8,128)S(1)}, u32[]{:S(2)}) copy-start(f32[128,128]{1,0:T(8,128)S(1)} %fusion.76) | copy-start | bytes 196612
  323.9 6.6 %copy-start.22 = (f32[384,128]{1,0:T(8,128)}, f32[384,128]{1,0:T(8,128)S(1)}, u32[]{:S(2)}) copy-start(f32[384,128]{1,0:T(8,128)S(1)} %get-tuple-element.70) | copy-start | bytes 589828
  332.3 81.1 %copy-start.17 = (f32[384,384]{1,0:T(8,128)}, f32[384,384]{1,0:T(8,128)S(1)}, u32[]{:S(2)}) copy-start(f32[384,384]{1,0:T(8,128)S(1)} %convolution_subtract_fusion.8) | copy-start | bytes 1769476
  332.3 80.2 %copy-start.2 = (f32[4,256,4,128]{1,3,2,0:T(8,128)S(1)}, f32[4,256,4,128]{1,3,2,0:T(8,128)}, u32[]{:S(2)}) copy-start(f32[4,256,4,128]{1,3,2,0:T(8,128)} %copy-done) | copy-start | bytes 6291460
  357.1 40.0 %copy-start.28 = (f32[128,128]{1,0:T(8,128)}, f32[128,128]{1,0:T(8,128)S(1)}, u32[]{:S(2)}) copy-start(f32[128,128]{1,0:T(8,128)S(1)} %fusion.70) | copy-start | bytes 196612
  358.1 39.0 %copy-start.24 = (f32[256,128]{1,0:T(8,128)}, f32[256,128]{1,0:T(8,128)S(1)}, u32[]{:S(2)}) copy-start(f32[256,128]{1,0:T(8,128)S(1)} %get-tuple-element.72) | copy-start | bytes 393220
  366.5 30.6 %copy-start.21 = (f32[256,256]{1,0:T(8,128)}, f32[256,256]{1,0:T(8,128)S(1)}, u32[]{:S(2)}) copy-start(f32[256,256]{1,0:T(8,128)S(1)} %convolution_subtract_fusion.11) | copy-start | bytes 786436
  397.1 10.4 %copy-start.30 = (f32[128,128]{1,0:T(8,128)}, f32[128,128]{1,0:T(8,128)S(1)}, u32[]{:S(2)}) copy-start(f32[128,128]{1,0:T(8,128)S(1)} %fusion.64) | copy-start | bytes 196612
  398.0 9.6 %copy-start.38 = (f32[128,128]{1,0:T(8,128)}, f32[128,128]{1,0:T(8,128)S(1)}, u32[]{:S(2)}) copy-start(f32[128,128]{1,0:T(8,128)S(1)} %get-tuple-element.74) | copy-start | bytes 196612
  398.0 16.8 %copy-start.8 = (f32[896,128]{1,0:T(8,128)S(1)}, f32[896,128]{1,0:T(8,128)}, u32[]{:S(2)}) copy-start(f32[896,128]{1,0:T(8,128)} %copy-done.6) | copy-start | bytes 1376260
  413.4 4.1 copy-start.15
  413.4 4.1 copy-start.12
  414.8 4.9 copy-start.20
  417.5 2.9 copy-start.23
  417.5 3.5 copy-start.25
  418.6 3.0 copy-start.39
  421.9 1.2 copy-start.16
  449.3 3.6 copy-start.41
  454.4 4.5 copy-start.33
  458.9 3.7 copy-start.35
  462.6 3.4 copy-start.37
  466.0 3.0 copy-start.27
  466.5 5.1 copy-start.29
  469.5 4.7 copy-start.31
  488.7 6.3 %copy-start.1 = (f32[4,256,4,128]{1,3,2,0:T(8,128)S(1)}, f32[4,256,4,128]{1,3,2,0:T(8,128)}, u32[]{:S(2)}) copy-start(f32[4,256,4,128]{1,3,2,0:T(8,128)} %copy-done) | copy-start | bytes 6291460
  496.7 7.8 %copy-start.4 = (f32[1,4,256,4,128]{2,4,3,1,0:T(8,128)S(1)}, f32[1,4,256,4,128]{2,4,3,1,0:T(8,128)}, u32[]{:S(2)}) copy-start(f32[1,4,256,4,128]{2,4,3,1,0:T(8,128)} %get-tuple-element.58) | copy-start | bytes 6291460
  499.6 17.8 %all-to-all-start.1 = ((f32[8,3,32,3,128]{4,2,3,1,0:T(8,128)}), f32[8,3,32,3,128]{4,2,3,1,0:T(8,128)S(1)}, u32[]{:S(2)}, u32[]{:S(2)}) async-start(f32[8,3,32,3,128]{4,2,3,1,0:T(8,128)} %copy.90), calls=%async_computation.1 | async-start | bytes 2359296 | tf_op jit(solution)/shard_map/all_to_all | solution.py:67
  (4 other events, 2.5 us)
Sparse Core Ops, SparseCore 0:
  44.0 27.1 all-gather.14
  78.5 14.1 all-gather.18
  94.5 40.8 all-gather.16
  137.1 43.7 all-gather.20
where the time goes:
time: 531 us; the launch traced here: 525 us
  other arithmetic  214 us (40%)
  local copies, waits for them, and re-layouts  92.3 us (17%)
  matrix products  77.4 us (15%)
  blocking collectives  74.1 us (14%)
  waiting for transfers between devices  42.2 us (8%)
  between operations  15.5 us (3%)
  starting transfers between devices  9.82 us (2%)
    another operation x24, other arithmetic, invert(): cholesky_factor = jnp.linalg.cholesky(gram_matrix)  105 us
    another operation x16, other arithmetic, invert(): return jax.scipy.linalg.cho_solve((cholesky_factor, True), pivot_tile.T)  91.4 us
    all_gather x6, blocking collectives, all_blocks(): tiles = lax.all_gather(tiles, axes[k], axis=0, tiled=True)  74.1 us
    dot_general x45, matrix products, full_dot(): jnp.dot(left, right, precision=lax.Precision.HIGHEST, preferred_element_t...  67.3 us
    unnamed x134, local copies, waits for them, and re-layouts  52.4 us
    all_to_all x1, waiting for transfers between devices, sent_to_all(): return lax.all_to_all(copies, axis, split_axis=0, concat_axis=0, tiled=True)  15.7 us
    all_gather x3, waiting for transfers between devices, all_blocks(): tiles = lax.all_gather(tiles, axes[k], axis=0, tiled=True)  15.3 us
    all_to_all x1, waiting for transfers between devices, summed_on_arrival(): lax.all_to_all(cut_along(shard, dim, length), axis, 0, 0, tiled=True)  11.1 us
  transfers between devices with their start and end apart: 6, of which 3 were waited for; matrix products, arithmetic and copies ran while one was open for 61% of the time, Pallas kernels for 0%

commit v1 on v0

--- a/solution.py
+++ b/solution.py
@@ -21,7 +21,9 @@
 def all_blocks(shard, axes, order):
     tiles = shard[None]
     for k in order:
-        tiles = lax.all_gather(tiles, axes[k], axis=0, tiled=True)
+        tiles = jnp.concatenate(
+            lax.all_to_all(jnp.stack([tiles] * lax.axis_size(axes[k])), axes[k], 0, 0), axis=0
+        )
     block = [lax.axis_size(axes[k]) for k in reversed(order)]
     tiles = tiles.reshape(*block, *shard.shape)
     turned = sorted(range(len(order)), key=lambda place: order[len(order) - 1 - place])

time: 531 us -> 593 us (1.12)
  waiting for transfers between devices: 42.2 us -> 112 us
  blocking collectives: 74.1 us -> 12.8 us
  starting transfers between devices: 9.82 us -> 50.9 us
  other arithmetic: 214 us -> 220 us
    all_to_all x0 -> x7, waiting for transfers between devices: none -> 80 us  [all_blocks(): lax.all_to_all(jnp.stack([tiles] * lax.axis_size(axes[k])), axes[k], 0, 0)]
    all_gather x6 -> x0, blocking collectives: 74.1 us -> none  [all_blocks(): tiles = lax.all_gather(tiles, axes[k], axis=0, tiled=True)]
    all_to_all x0 -> x7, starting transfers between devices: none -> 38 us  [all_blocks(): lax.all_to_all(jnp.stack([tiles] * lax.axis_size(axes[k])), axes[k], 0, 0)]
    all_gather x3 -> x0, waiting for transfers between devices: 15.3 us -> none  [all_blocks(): tiles = lax.all_gather(tiles, axes[k], axis=0, tiled=True)]
    all_to_all x0 -> x2, blocking collectives: none -> 12.8 us  [all_blocks(): lax.all_to_all(jnp.stack([tiles] * lax.axis_size(axes[k])), axes[k], 0, 0)]
    unnamed x134 -> x136, local copies, waits for them, and re-layouts: 52.4 us -> 52.7 us
  transfers between devices with their start and end apart: 6 -> 10, of which waited for: 3 -> 9; matrix products, arithmetic and copies ran while one was open for 61% -> 55% of each run, Pallas kernels for 0% -> 0%
where the time goes in v1:
time: 593 us; the launch traced here: 584 us
  other arithmetic  220 us (37%)
  waiting for transfers between devices  112 us (19%)
  local copies, waits for them, and re-layouts  94.6 us (16%)
  matrix products  77.2 us (13%)
  starting transfers between devices  50.9 us (9%)
  between operations  15.8 us (3%)
  blocking collectives  12.8 us (2%)
    another operation x24, other arithmetic, invert(): cholesky_factor = jnp.linalg.cholesky(gram_matrix)  105 us
    another operation x16, other arithmetic, invert(): return jax.scipy.linalg.cho_solve((cholesky_factor, True), pivot_tile.T)  91.4 us
    all_to_all x7, waiting for transfers between devices, all_blocks(): lax.all_to_all(jnp.stack([tiles] * lax.axis_size(axes[k])), axes[k], 0, 0)  80 us
    dot_general x45, matrix products, full_dot(): jnp.dot(left, right, precision=lax.Precision.HIGHEST, preferred_element_t...  67.3 us
    unnamed x136, local copies, waits for them, and re-layouts  52.7 us
    all_to_all x7, starting transfers between devices, all_blocks(): lax.all_to_all(jnp.stack([tiles] * lax.axis_size(axes[k])), axes[k], 0, 0)  38 us
    all_to_all x1, waiting for transfers between devices, sent_to_all(): return lax.all_to_all(copies, axis, split_axis=0, concat_axis=0, tiled=True)  17.2 us
    all_to_all x1, waiting for transfers between devices, summed_on_arrival(): lax.all_to_all(cut_along(shard, dim, length), axis, 0, 0, tiled=True)  14.9 us
  transfers between devices with their start and end apart: 10, of which 9 were waited for; matrix products, arithmetic and copies ran while one was open for 55% of the time, Pallas kernels for 0%

profile of v1, /device:TPU:16, one launch (start us, length us, event | category | flops | bytes accessed | tf_op | source)
XLA Modules:
  0.0 583.7 jit_solution(5743871851725914760)
XLA Ops:
  7.2 2.9 copy.63
  13.5 3.3 all-to-all-start.3
  18.2 5.4 all-to-all-start.6
  26.6 7.9 %all-to-all-start = ((f32[8,1,1,80,128]{4,3,2,1,0:T(8,128)}), f32[8,1,1,80,128]{4,3,2,1,0:T(8,128)S(1)}, u32[]{:S(2)}, u32[]{:S(2)}) async-start(f32[8,1,1,80,128]{4,3,2,1,0:T(8,128)} %stack.27), calls=%async_computation | async-start | bytes 655360 | tf_op jit(solution)/shard_map/all_to_all | solution.py:25
  35.2 11.8 %all-to-all-done = f32[8,1,1,80,128]{4,3,2,1,0:T(8,128)S(1)} async-done(((f32[8,1,1,80,128]{4,3,2,1,0:T(8,128)}), f32[8,1,1,80,128]{4,3,2,1,0:T(8,128)S(1)}, u32[]{:S(2)}, u32[]{:S(2)}) %all-to-all-start) | async-done | bytes 327712 | tf_op jit(solution)/shard_map/all_to_all | solution.py:25
  47.0 6.7 %all-to-all-start.4 = ((f32[2,2,1,80,128]{4,3,2,1,0:T(8,128)}), f32[2,2,1,80,128]{4,3,2,1,0:T(8,128)S(1)}, u32[]{:S(2)}, u32[]{:S(2)}) async-start(f32[2,2,1,80,128]{4,3,2,1,0:T(8,128)} %maximum_bitcast_fusion.1), calls=%async_computation.4 | async-start | bytes 327680 | tf_op jit(solution)/shard_map/all_to_all | solution.py:25
  53.7 2.6 all-to-all-done.4
  56.3 5.0 all_to_all.55
  62.3 3.5 all-to-all-start.7
  65.9 23.6 %all-to-all-done.7 = f32[8,2,1,96,128]{4,3,1,2,0:T(8,128)S(1)} async-done(((f32[8,2,1,96,128]{4,3,1,2,0:T(8,128)}), f32[8,2,1,96,128]{4,3,1,2,0:T(8,128)S(1)}, u32[]{:S(2)}, u32[]{:S(2)}) %all-to-all-start.7) | async-done | bytes 786464 | tf_op jit(solution)/shard_map/all_to_all | solution.py:25
  90.8 7.8 %all-to-all-start.9 = ((f32[4,256,3,128]{1,3,2,0:T(8,128)}), f32[4,256,3,128]{1,3,2,0:T(8,128)}, u32[]{:S(2)}, u32[]{:S(2)}) async-start(f32[4,256,3,128]{1,3,2,0:T(8,128)} %broadcast_in_dim.24), calls=%async_computation.9 | async-start | bytes 3145728 | tf_op jit(solution)/shard_map/all_to_all | solution.py:53
  100.0 17.2 %all-to-all-done.9 = f32[4,256,3,128]{1,3,2,0:T(8,128)} async-done(((f32[4,256,3,128]{1,3,2,0:T(8,128)}), f32[4,256,3,128]{1,3,2,0:T(8,128)}, u32[]{:S(2)}, u32[]{:S(2)}) %all-to-all-start.9) | async-done | bytes 1572896 | tf_op jit(solution)/shard_map/all_to_all | solution.py:53
  117.1 7.8 %all_to_all.56 = f32[2,16,1,96,128]{4,3,1,2,0:T(8,128)} all-to-all(f32[2,16,1,96,128]{4,3,1,2,0:T(8,128)} %pad_maximum_fusion), channel_id=1, replica_groups=mesh['layer'=8,'prow_0'=2,'prow_1'=2,'pcol'=8] {'prow_1'}, dimensions={0} | all-to-all | bytes 3145728 | tf_op jit(solution)/shard_map/all_to_all | solution.py:25
  126.1 3.6 all-to-all-start.5
  129.7 2.5 pad_maximum_fusion.1
  132.2 32.4 %all-to-all-done.5 = f32[8,4,1,80,128]{4,3,1,2,0:T(8,128)S(1)} async-done(((f32[8,4,1,80,128]{4,3,1,2,0:T(8,128)}), f32[8,4,1,80,128]{4,3,1,2,0:T(8,128)S(1)}, u32[]{:S(2)}, u32[]{:S(2)}) %all-to-all-start.5) | async-done | bytes 1310752 | tf_op jit(solution)/shard_map/all_to_all | solution.py:25
  164.5 7.7 %all-to-all-start.2 = ((f32[2,16,1,80,128]{4,3,1,2,0:T(8,128)}), f32[2,16,1,80,128]{4,3,1,2,0:T(8,128)}, u32[]{:S(2)}, u32[]{:S(2)}) async-start(f32[2,16,1,80,128]{4,3,1,2,0:T(8,128)} %pad_maximum_fusion.1), calls=%async_computation.2 | async-start | bytes 2621440 | tf_op jit(solution)/shard_map/all_to_all | solution.py:25
  180.6 6.9 %all-to-all-done.2 = f32[2,16,1,80,128]{4,3,1,2,0:T(8,128)} async-done(((f32[2,16,1,80,128]{4,3,1,2,0:T(8,128)}), f32[2,16,1,80,128]{4,3,1,2,0:T(8,128)}, u32[]{:S(2)}, u32[]{:S(2)}) %all-to-all-start.2) | async-done | bytes 1310752 | tf_op jit(solution)/shard_map/all_to_all | solution.py:25
  189.6 2.4 copy.72
  195.4 11.7 %cholesky.134 = f32[128,128]{1,0:T(8,128)S(1)} custom-call(f32[128,128]{1,0:T(8,128)S(1)} %fusion.103), custom_call_target="Cholesky" | custom-call | tf_op jit(solution)/shard_map/jit(cholesky)/cholesky | solution.py:79
  208.5 9.8 %custom-call.14 = f32[1,128,128]{1,2,0:T(8,128)S(1)} custom-call(f32[1,128,128]{2,1,0:T(8,128)S(1)} %fusion.46), custom_call_target="InvertDiagBlocksLowerTriangular" | custom-call | tf_op jit(solution)/shard_map/jit(_cho_solve)/triangular_solve | solution.py:80
  222.6 5.2 slice_subtract_fusion
  230.0 11.7 %cholesky.145 = f32[128,128]{1,0:T(8,128)S(1)} custom-call(f32[128,128]{1,0:T(8,128)S(1)} %fusion.97), custom_call_target="Cholesky" | custom-call | tf_op jit(solution)/shard_map/jit(cholesky)/cholesky | solution.py:79
  243.0 9.8 %custom-call.15 = f32[1,128,128]{1,2,0:T(8,128)S(1)} custom-call(f32[1,128,128]{2,1,0:T(8,128)S(1)} %fusion.47), custom_call_target="InvertDiagBlocksLowerTriangular" | custom-call | tf_op jit(solution)/shard_map/jit(_cho_solve)/triangular_solve | solution.py:80
  259.6 11.9 %cholesky.156 = f32[128,128]{1,0:T(8,128)S(1)} custom-call(f32[128,128]{1,0:T(8,128)S(1)} %fusion.91), custom_call_target="Cholesky" | custom-call | tf_op jit(solution)/shard_map/jit(cholesky)/cholesky | solution.py:79
  272.7 9.8 %custom-call.16 = f32[1,128,128]{1,2,0:T(8,128)S(1)} custom-call(f32[1,128,128]{2,1,0:T(8,128)S(1)} %fusion.48), custom_call_target="InvertDiagBlocksLowerTriangular" | custom-call | tf_op jit(solution)/shard_map/jit(_cho_solve)/triangular_solve | solution.py:80
  285.9 3.0 slice_subtract_fusion.5
  300.8 13.2 %cholesky.167 = f32[128,128]{1,0:T(8,128)} custom-call(f32[128,128]{1,0:T(8,128)} %fusion.85), custom_call_target="Cholesky" | custom-call | tf_op jit(solution)/shard_map/jit(cholesky)/cholesky | solution.py:79
  317.7 11.4 %custom-call.17 = f32[1,128,128]{1,2,0:T(8,128)} custom-call(f32[1,128,128]{2,1,0:T(8,128)} %fusion.49), custom_call_target="InvertDiagBlocksLowerTriangular" | custom-call | tf_op jit(solution)/shard_map/jit(_cho_solve)/triangular_solve | solution.py:80
  345.6 13.2 %cholesky.178 = f32[128,128]{1,0:T(8,128)} custom-call(f32[128,128]{1,0:T(8,128)} %fusion.79), custom_call_target="Cholesky" | custom-call | tf_op jit(solution)/shard_map/jit(cholesky)/cholesky | solution.py:79
  362.4 11.3 %custom-call.18 = f32[1,128,128]{1,2,0:T(8,128)} custom-call(f32[1,128,128]{2,1,0:T(8,128)} %fusion.50), custom_call_target="InvertDiagBlocksLowerTriangular" | custom-call | tf_op jit(solution)/shard_map/jit(_cho_solve)/triangular_solve | solution.py:80
  387.4 12.1 %cholesky.189 = f32[128,128]{1,0:T(8,128)S(1)} custom-call(f32[128,128]{1,0:T(8,128)S(1)} %fusion.73), custom_call_target="Cholesky" | custom-call | tf_op jit(solution)/shard_map/jit(cholesky)/cholesky | solution.py:79
  400.9 9.8 %custom-call.19 = f32[1,128,128]{1,2,0:T(8,128)S(1)} custom-call(f32[1,128,128]{2,1,0:T(8,128)S(1)} %fusion.51), custom_call_target="InvertDiagBlocksLowerTriangular" | custom-call | tf_op jit(solution)/shard_map/jit(_cho_solve)/triangular_solve | solution.py:80
  423.8 12.5 %cholesky.200 = f32[128,128]{1,0:T(8,128)S(1)} custom-call(f32[128,128]{1,0:T(8,128)} %fusion.67), custom_call_target="Cholesky" | custom-call | tf_op jit(solution)/shard_map/jit(cholesky)/cholesky | solution.py:79
  438.3 10.8 %custom-call.20 = f32[1,128,128]{1,2,0:T(8,128)S(1)} custom-call(f32[1,128,128]{2,1,0:T(8,128)} %fusion.52), custom_call_target="InvertDiagBlocksLowerTriangular" | custom-call | tf_op jit(solution)/shard_map/jit(_cho_solve)/triangular_solve | solution.py:80
  468.8 2.7 convolution_subtract_fusion
  477.8 11.7 %cholesky.211 = f32[128,128]{1,0:T(8,128)S(1)} custom-call(f32[128,128]{1,0:T(8,128)S(1)} %fusion.61), custom_call_target="Cholesky" | custom-call | tf_op jit(solution)/shard_map/jit(cholesky)/cholesky | solution.py:79
  490.8 10.0 %custom-call.21 = f32[1,128,128]{1,2,0:T(8,128)S(1)} custom-call(f32[1,128,128]{2,1,0:T(8,128)S(1)} %fusion.53), custom_call_target="InvertDiagBlocksLowerTriangular" | custom-call | tf_op jit(solution)/shard_map/jit(_cho_solve)/triangular_solve | solution.py:80
  503.5 3.5 copy.85
  508.6 4.5 slice_subtract_fusion.1
  513.6 3.2 slice_subtract_fusion.2
  517.3 2.8 slice_subtract_fusion.4
  520.7 2.4 slice_subtract_fusion.6
  531.1 2.4 copy.87
  533.4 7.5 %fusion.130 = f32[768,384]{1,0:T(8,128)} fusion(f32[768,1024]{0,1:T(8,128)S(1)} %convolution_dynamic-update-slice_fusion, f32[1024,384]{1,0:T(8,128)} %copy-done.17), kind=kOutput, calls=%fused_computation.262 | convolution fusion | flops 3623878656 | bytes 5898240 | tf_op jit(solution)/shard_map/dot_general | solution.py:74
  542.9 3.0 reshape.237
  553.9 5.1 all-to-all-start.10
  560.8 14.9 %all-to-all-done.10 = f32[8,3,32,3,128]{4,2,3,1,0:T(8,128)S(1)} async-done(((f32[8,3,32,3,128]{4,2,3,1,0:T(8,128)}), f32[8,3,32,3,128]{4,2,3,1,0:T(8,128)S(1)}, u32[]{:S(2)}, u32[]{:S(2)}) %all-to-all-start.10) | async-done | bytes 1179680 | tf_op jit(solution)/shard_map/all_to_all | solution.py:69
  (283 shorter events, 166.2 us)
Async XLA Ops:
  7.2 2.9 copy-start.45
  12.4 160.6 %copy-start = (f32[4,256,4,128]{1,3,2,0:T(8,128)}, f32[4,256,4,128]{1,3,2,0:T(8,128)S(1)}, u32[]{:S(2)}) copy-start(f32[4,256,4,128]{1,3,2,0:T(8,128)S(1)} %bitcast_multiply_fusion) | copy-start | bytes 6291460
  13.5 4.7 all-to-all-start.3
  18.2 7.7 %all-to-all-start.6 = ((f32[2,1,1,96,128]{4,3,2,1,0:T(8,128)}), f32[2,1,1,96,128]{4,3,2,1,0:T(8,128)S(1)}, u32[]{:S(2)}, u32[]{:S(2)}) async-start(f32[2,1,1,96,128]{4,3,2,1,0:T(8,128)} %copy.70), calls=%async_computation.6 | async-start | bytes 196608 | tf_op jit(solution)/shard_map/all_to_all | solution.py:25
  26.6 20.3 %all-to-all-start = ((f32[8,1,1,80,128]{4,3,2,1,0:T(8,128)}), f32[8,1,1,80,128]{4,3,2,1,0:T(8,128)S(1)}, u32[]{:S(2)}, u32[]{:S(2)}) async-start(f32[8,1,1,80,128]{4,3,2,1,0:T(8,128)} %stack.27), calls=%async_computation | async-start | bytes 655360 | tf_op jit(solution)/shard_map/all_to_all | solution.py:25
  47.0 9.3 %all-to-all-start.4 = ((f32[2,2,1,80,128]{4,3,2,1,0:T(8,128)}), f32[2,2,1,80,128]{4,3,2,1,0:T(8,128)S(1)}, u32[]{:S(2)}, u32[]{:S(2)}) async-start(f32[2,2,1,80,128]{4,3,2,1,0:T(8,128)} %maximum_bitcast_fusion.1), calls=%async_computation.4 | async-start | bytes 327680 | tf_op jit(solution)/shard_map/all_to_all | solution.py:25
  62.3 27.2 %all-to-all-start.7 = ((f32[8,2,1,96,128]{4,3,1,2,0:T(8,128)}), f32[8,2,1,96,128]{4,3,1,2,0:T(8,128)S(1)}, u32[]{:S(2)}, u32[]{:S(2)}) async-start(f32[8,2,1,96,128]{4,3,1,2,0:T(8,128)} %stack.34), calls=%async_computation.7 | async-start | bytes 1572864 | tf_op jit(solution)/shard_map/all_to_all | solution.py:25
  90.8 26.3 %all-to-all-start.9 = ((f32[4,256,3,128]{1,3,2,0:T(8,128)}), f32[4,256,3,128]{1,3,2,0:T(8,128)}, u32[]{:S(2)}, u32[]{:S(2)}) async-start(f32[4,256,3,128]{1,3,2,0:T(8,128)} %broadcast_in_dim.24), calls=%async_computation.9 | async-start | bytes 3145728 | tf_op jit(solution)/shard_map/all_to_all | solution.py:53
  126.1 38.4 %all-to-all-start.5 = ((f32[8,4,1,80,128]{4,3,1,2,0:T(8,128)}), f32[8,4,1,80,128]{4,3,1,2,0:T(8,128)S(1)}, u32[]{:S(2)}, u32[]{:S(2)}) async-start(f32[8,4,1,80,128]{4,3,1,2,0:T(8,128)} %stack.32), calls=%async_computation.5 | async-start | bytes 2621440 | tf_op jit(solution)/shard_map/all_to_all | solution.py:25
  164.5 22.9 %all-to-all-start.2 = ((f32[2,16,1,80,128]{4,3,1,2,0:T(8,128)}), f32[2,16,1,80,128]{4,3,1,2,0:T(8,128)}, u32[]{:S(2)}, u32[]{:S(2)}) async-start(f32[2,16,1,80,128]{4,3,1,2,0:T(8,128)} %pad_maximum_fusion.1), calls=%async_computation.2 | async-start | bytes 2621440 | tf_op jit(solution)/shard_map/all_to_all | solution.py:25
  172.2 331.3 %all-gather.3.cloned.1.call-start = ((), (), s32[]{:S(2)}) async-start(), calls=%async_computation.11 | async-start | bytes 3538944 | tf_op jit(solution)/shard_map/all_gather | solution.py:160
  177.3 2.0 copy-start.10
  177.4 2.0 copy-start.19
  193.0 2.0 copy-start.3
  227.7 151.7 %copy-start.5 = (f32[896,896]{1,0:T(8,128)}, f32[896,896]{1,0:T(8,128)S(1)}, u32[]{:S(2)}) copy-start(f32[896,896]{1,0:T(8,128)S(1)} %slice_subtract_fusion) | copy-start | bytes 9633796
  252.8 5.8 copy-start.7
  254.4 4.2 copy-start.11
  282.5 6.4 %copy-start.12 = (f32[768,128]{1,0:T(8,128)S(1)}, f32[768,128]{1,0:T(8,128)}, u32[]{:S(2)}) copy-start(f32[768,128]{1,0:T(8,128)} %copy-done.11) | copy-start | bytes 1179652
  282.5 8.3 %copy-start.44 = (f32[128,128]{1,0:T(8,128)S(1)}, f32[128,128]{1,0:T(8,128)}, u32[]{:S(2)}) copy-start(f32[128,128]{1,0:T(8,128)} %slice.544) | copy-start | bytes 196612
  288.9 8.2 %copy-start.14 = (f32[640,640]{1,0:T(8,128)}, f32[640,640]{1,0:T(8,128)S(1)}, u32[]{:S(2)}) copy-start(f32[640,640]{1,0:T(8,128)S(1)} %slice_subtract_fusion.5) | copy-start | bytes 4915204
  331.4 7.2 %copy-start.37 = (f32[128,128]{1,0:T(8,128)}, f32[128,128]{1,0:T(8,128)S(1)}, u32[]{:S(2)}) copy-start(f32[128,128]{1,0:T(8,128)S(1)} %fusion.82) | copy-start | bytes 196612
  333.4 5.2 copy-start.20
  375.9 8.6 %copy-start.27 = (f32[128,128]{1,0:T(8,128)}, f32[128,128]{1,0:T(8,128)S(1)}, u32[]{:S(2)}) copy-start(f32[128,128]{1,0:T(8,128)S(1)} %fusion.76) | copy-start | bytes 196612
  377.9 6.6 %copy-start.23 = (f32[384,128]{1,0:T(8,128)}, f32[384,128]{1,0:T(8,128)S(1)}, u32[]{:S(2)}) copy-start(f32[384,128]{1,0:T(8,128)S(1)} %get-tuple-element.70) | copy-start | bytes 589828
  386.3 81.1 %copy-start.18 = (f32[384,384]{1,0:T(8,128)}, f32[384,384]{1,0:T(8,128)S(1)}, u32[]{:S(2)}) copy-start(f32[384,384]{1,0:T(8,128)S(1)} %convolution_subtract_fusion.8) | copy-start | bytes 1769476
  386.3 80.2 %copy-start.2 = (f32[4,256,4,128]{1,3,2,0:T(8,128)S(1)}, f32[4,256,4,128]{1,3,2,0:T(8,128)}, u32[]{:S(2)}) copy-start(f32[4,256,4,128]{1,3,2,0:T(8,128)} %copy-done) | copy-start | bytes 6291460
  411.2 39.9 %copy-start.29 = (f32[128,128]{1,0:T(8,128)}, f32[128,128]{1,0:T(8,128)S(1)}, u32[]{:S(2)}) copy-start(f32[128,128]{1,0:T(8,128)S(1)} %fusion.70) | copy-start | bytes 196612
  412.1 39.0 %copy-start.25 = (f32[256,128]{1,0:T(8,128)}, f32[256,128]{1,0:T(8,128)S(1)}, u32[]{:S(2)}) copy-start(f32[256,128]{1,0:T(8,128)S(1)} %get-tuple-element.72) | copy-start | bytes 393220
  420.7 30.5 %copy-start.22 = (f32[256,256]{1,0:T(8,128)}, f32[256,256]{1,0:T(8,128)S(1)}, u32[]{:S(2)}) copy-start(f32[256,256]{1,0:T(8,128)S(1)} %convolution_subtract_fusion.11) | copy-start | bytes 786436
  451.1 10.4 %copy-start.31 = (f32[128,128]{1,0:T(8,128)}, f32[128,128]{1,0:T(8,128)S(1)}, u32[]{:S(2)}) copy-start(f32[128,128]{1,0:T(8,128)S(1)} %fusion.64) | copy-start | bytes 196612
  452.0 9.6 %copy-start.39 = (f32[128,128]{1,0:T(8,128)}, f32[128,128]{1,0:T(8,128)S(1)}, u32[]{:S(2)}) copy-start(f32[128,128]{1,0:T(8,128)S(1)} %get-tuple-element.74) | copy-start | bytes 196612
  452.0 16.8 %copy-start.8 = (f32[896,128]{1,0:T(8,128)S(1)}, f32[896,128]{1,0:T(8,128)}, u32[]{:S(2)}) copy-start(f32[896,128]{1,0:T(8,128)} %copy-done.6) | copy-start | bytes 1376260
  467.5 4.1 copy-start.16
  467.5 4.1 copy-start.13
  468.8 4.9 copy-start.21
  471.6 2.9 copy-start.24
  471.6 3.5 copy-start.26
  472.7 3.0 copy-start.40
  503.5 3.6 copy-start.42
  508.6 4.5 copy-start.34
  513.1 3.7 copy-start.36
  516.8 3.4 copy-start.38
  520.2 3.0 copy-start.28
  520.7 5.1 copy-start.30
  523.7 4.7 copy-start.32
  542.9 6.4 %copy-start.1 = (f32[4,256,4,128]{1,3,2,0:T(8,128)S(1)}, f32[4,256,4,128]{1,3,2,0:T(8,128)}, u32[]{:S(2)}) copy-start(f32[4,256,4,128]{1,3,2,0:T(8,128)} %copy-done) | copy-start | bytes 6291460
  551.0 8.0 %copy-start.4 = (f32[1,4,256,4,128]{2,4,3,1,0:T(8,128)S(1)}, f32[1,4,256,4,128]{2,4,3,1,0:T(8,128)}, u32[]{:S(2)}) copy-start(f32[1,4,256,4,128]{2,4,3,1,0:T(8,128)} %get-tuple-element.58) | copy-start | bytes 6291460
  553.9 21.8 %all-to-all-start.10 = ((f32[8,3,32,3,128]{4,2,3,1,0:T(8,128)}), f32[8,3,32,3,128]{4,2,3,1,0:T(8,128)S(1)}, u32[]{:S(2)}, u32[]{:S(2)}) async-start(f32[8,3,32,3,128]{4,2,3,1,0:T(8,128)} %copy.91), calls=%async_computation.10 | async-start | bytes 2359296 | tf_op jit(solution)/shard_map/all_to_all | solution.py:69
  (9 other events, 8.4 us)
Sparse Core Ops, SparseCore 0:
  174.8 41.3 all-gather.2
